TPU v7x, 256 devices: a whole 4x4x8 slice. The times are simulated.
256 devices in a mesh: rep: 8 (over x, z_lo), mp: 32 (over z_hi, y, core).
Axes of the slice: x: 4, y: 4, z: 8 (z_hi: 4, z_lo: 2; z = z_hi * 2 + z_lo), core: 2. Of those that a mesh axis runs over, the one named last changes fastest.
Arguments:
- tokens: bfloat16 [8, 2048, 5120], P('rep', 'mp'), may hold values from -6 to 6
- prompt_ids: int32 [8, 2048], P('rep', 'mp'), may hold values from 0 to 11, never falling along the last dimension, each value on 1 to 512 neighbouring positions
- modulation: float32 [8, 12, 3, 5120], P('rep'), may hold values from -4 to 4
- trainer_up: float32 [5120, 13824], P('mp', 'rep'), may hold values from -0.078125 to 0.078125
- trainer_down: float32 [13824, 5120], P('rep', 'mp'), may hold values from -0.0546875 to 0.0546875
Outputs:
- result: bfloat16 [8, 2048, 5120], P('rep', 'mp')
Inputs may be any that keep to these rules, and one draw needn't show every extreme that they name: `prompt_ids`: along each replica's 2048 tokens the prompt number never falls; each of the 12 prompts has at least one token, and one prompt has exactly a quarter of 2048.
All inputs are finite; a program needn't handle non-finite values.
Results may differ from a plain program's by a relative error of at most 0.023.
Values may be sent and summed in bfloat16 or wider, within the bound.
A program may use at most 192 MiB of HBM per device.

v0:
```python
import jax
import jax.numpy as jnp
from jax import lax
from jax.sharding import PartitionSpec as P


def local(tokens, prompt_ids, modulation, trainer_up, trainer_down):
    as_float = tokens[0].astype(jnp.float32)
    average = jnp.mean(as_float, axis=-1, keepdims=True)
    centred = as_float - average
    variance = jnp.mean(centred * centred, axis=-1, keepdims=True)
    normed = centred / jnp.sqrt(variance + 1e-06)
    prompts_here = modulation.shape[1]
    onehot = (prompt_ids[0][:, None] == jnp.arange(prompts_here, dtype=jnp.int32)[None, :]).astype(
        jnp.float32
    )
    chosen = jnp.einsum("tp,pkd->tkd", onehot, modulation[0], precision=lax.Precision.HIGHEST)
    shift = chosen[:, 0]
    scale = chosen[:, 1]
    gate = chosen[:, 2]
    xin = (normed * (1.0 + scale) + shift).astype(jnp.bfloat16)
    up_half = trainer_up.astype(jnp.bfloat16)
    down_half = trainer_down.astype(jnp.bfloat16)
    up_rows = lax.all_gather(up_half, "rep", axis=1, tiled=True)
    w_up = lax.all_to_all(up_rows, "mp", split_axis=1, concat_axis=0, tiled=True)
    down_columns = lax.all_gather(down_half, "rep", axis=0, tiled=True)
    w_down = lax.all_to_all(down_columns, "mp", split_axis=0, concat_axis=1, tiled=True)
    hidden = jax.nn.gelu(
        jnp.dot(
            lax.all_gather(xin, "mp", axis=0, tiled=True), w_up, preferred_element_type=jnp.float32
        ),
        approximate=True,
    ).astype(jnp.bfloat16)
    mlp = lax.psum_scatter(
        jnp.dot(hidden, w_down, preferred_element_type=jnp.float32).astype(jnp.bfloat16),
        "mp",
        scatter_dimension=0,
        tiled=True,
    ).astype(jnp.float32)
    result = as_float + gate * mlp
    return result.astype(jnp.bfloat16)[None]


def solution(mesh):
    in_specs = (
        P("rep", "mp", None),
        P("rep", "mp"),
        P("rep", None, None, None),
        P("mp", "rep"),
        P("rep", "mp"),
    )
    out_specs = P("rep", "mp", None)
    return jax.shard_map(local, mesh=mesh, in_specs=in_specs, out_specs=out_specs, check_vma=False)
```

profile of v0, /device:TPU:1, one launch (start us, length us, event | category | flops | bytes accessed | tf_op | source)
XLA Modules:
  0.0 793.0 jit_solution(6808156185871499909)
XLA Ops:
  6.5 2.2 convert_bitcast_fusion.2
  8.8 2.1 convert_bitcast_fusion.1
  11.1 0.2 convert_reduce_fusion
  11.3 0.3 fusion.17
  11.6 1.8 fusion.24
  13.4 1.9 copy-done
  15.3 1.2 fusion.23
  16.5 96.8 %all-gather.8.cloned.1.call-done = bf16[8,1728,160]{1,2,0:T(8,128)(2,1)} async-done(((bf16[1,1728,160]{1,2,0:T(8,128)(2,1)}), bf16[8,1728,160]{1,2,0:T(8,128)(2,1)}) %all-gather.8.cloned.1.call-update) | async-done | bytes 4423696 | tf_op jit(solution)/shard_map/all_gather | solution.py:24
  113.3 7.0 copy.13
  120.3 8.6 %reshape.23 = bf16[13824,160]{0,1:T(8,128)(2,1)} reshape(bf16[8,1728,160]{1,0,2:T(8,128)(2,1)} %copy.13) | data formatting | bytes 8847360
  128.9 13.7 %all_to_all.28 = bf16[160,32,432]{2,1,0:T(8,128)(2,1)} reshape(bf16[160,13824]{1,0:T(8,128)(2,1)} %bitcast.79) | data formatting | bytes 8847360 | tf_op jit(solution)/shard_map/all_to_all | solution.py:25
  142.6 7.8 copy.14
  150.4 9.7 %all-to-all-start = ((bf16[160,32,432]{2,0,1:T(8,128)(2,1)}), bf16[160,32,432]{2,0,1:T(8,128)(2,1)}, u32[]{:S(2)}, u32[]{:S(2)}) async-start(bf16[160,32,432]{2,0,1:T(8,128)(2,1)} %copy.14), calls=%async_computation | async-start | bytes 10485760 | tf_op jit(solution)/shard_map/all_to_all | solution.py:25
  160.1 158.4 %all-gather.10.cloned.1.call-done = bf16[8,1728,160]{1,2,0:T(8,128)(2,1)} async-done(((bf16[1,1728,160]{1,2,0:T(8,128)(2,1)}), bf16[8,1728,160]{1,2,0:T(8,128)(2,1)}) %all-gather.10.cloned.1.call-update) | async-done | bytes 4423696 | tf_op jit(solution)/shard_map/all_gather | solution.py:26
  318.6 6.9 copy.15
  325.4 10.6 %all_to_all.32 = bf16[32,432,160]{1,0,2:T(8,128)(2,1)} reshape(bf16[8,1728,160]{1,0,2:T(8,128)(2,1)} %copy.15) | data formatting | bytes 8847360 | tf_op jit(solution)/shard_map/all_to_all | solution.py:27
  336.0 7.9 %copy.16 = bf16[32,432,160]{1,2,0:T(8,128)(2,1)} copy(bf16[32,432,160]{1,0,2:T(8,128)(2,1)} %all_to_all.32) | data formatting | bytes 8847360 | tf_op jit(solution)/shard_map/all_to_all | solution.py:27
  344.0 11.5 %all-to-all-start.1 = ((bf16[32,432,160]{1,2,0:T(8,128)(2,1)}), bf16[32,432,160]{1,2,0:T(8,128)(2,1)}, u32[]{:S(2)}, u32[]{:S(2)}) async-start(bf16[32,432,160]{1,2,0:T(8,128)(2,1)} %copy.16), calls=%async_computation.1 | async-start | bytes 10485760 | tf_op jit(solution)/shard_map/all_to_all | solution.py:27
  355.5 0.3 reduce-scatter.2.cloned.1.call-start
  355.8 208.1 %all-gather.6.cloned.1.call-done = bf16[2048,5120]{1,0:T(8,128)(2,1)} async-done(((bf16[64,5120]{1,0:T(8,128)(2,1)}), bf16[2048,5120]{1,0:T(8,128)(2,1)}) %all-gather.6.cloned.1.call-update) | async-done | bytes 20971536 | tf_op jit(solution)/shard_map/all_gather | solution.py:30
  563.9 15.8 %fusion.49 = bf16[2048,432]{0,1:T(8,128)(2,1)S(1)} fusion(bf16[2048,5120]{1,0:T(8,128)(2,1)} %all-gather.6.cloned.1.call-done, bf16[5120,432]{1,0:T(8,128)(2,1)} %bitcast.11), kind=kOutput, calls=%fused_computation.9.clone.clone.1 | convolution fusion | flops 9067659264 | bytes 27164672 | tf_op jit(solution)/shard_map/dot_general | solution.py:29
  579.7 16.8 %convolution_convert_fusion = bf16[2048,5120]{1,0:T(8,128)(2,1)} fusion(bf16[432,5120]{0,1:T(8,128)(2,1)} %bitcast.14, bf16[2048,432]{0,1:T(8,128)(2,1)S(1)} %fusion.49), kind=kOutput, calls=%fused_computation | convolution fusion | flops 9070182400 | bytes 27164672 | tf_op jit(solution)/shard_map/dot_general | solution.py:35
  596.5 187.5 %reduce-scatter.2.cloned.1.call-done = bf16[64,5120]{1,0:T(8,128)(2,1)} async-done(((bf16[2048,5120]{1,0:T(8,128)(2,1)}), bf16[64,5120]{1,0:T(8,128)(2,1)}) %reduce-scatter.2.cloned.1.call-update) | async-done | bytes 655376 | tf_op jit(solution)/shard_map/reduce_scatter | solution.py:34
  783.9 2.6 fusion.27
  (18 shorter events, 0.2 us)
Async XLA Ops:
  6.5 4.5 copy-start.1
  6.5 5.1 copy-start.3
  6.5 5.1 copy-start.2
  6.5 106.8 %all-gather.8.cloned.1.call-start = ((), (), s32[]{:S(2)}) async-start(), calls=%async_computation.5 | async-start | bytes 5160960 | tf_op jit(solution)/shard_map/all_gather | solution.py:24
  8.8 309.8 %all-gather.10.cloned.1.call-start = ((), (), s32[]{:S(2)}) async-start(), calls=%async_computation.6 | async-start | bytes 5160960 | tf_op jit(solution)/shard_map/all_gather | solution.py:26
  11.0 552.9 %all-gather.6.cloned.1.call-start = ((), (), s32[]{:S(2)}) async-start(), calls=%async_computation.3 | async-start | bytes 21626880 | tf_op jit(solution)/shard_map/all_gather | solution.py:30
  13.4 1.9 copy-start
  150.4 193.6 %all-to-all-start = ((bf16[160,32,432]{2,0,1:T(8,128)(2,1)}), bf16[160,32,432]{2,0,1:T(8,128)(2,1)}, u32[]{:S(2)}, u32[]{:S(2)}) async-start(bf16[160,32,432]{2,0,1:T(8,128)(2,1)} %copy.14), calls=%async_computation | async-start | bytes 10485760 | tf_op jit(solution)/shard_map/all_to_all | solution.py:25
  344.0 235.7 %all-to-all-start.1 = ((bf16[32,432,160]{1,2,0:T(8,128)(2,1)}), bf16[32,432,160]{1,2,0:T(8,128)(2,1)}, u32[]{:S(2)}, u32[]{:S(2)}) async-start(bf16[32,432,160]{1,2,0:T(8,128)(2,1)} %copy.16), calls=%async_computation.1 | async-start | bytes 10485760 | tf_op jit(solution)/shard_map/all_to_all | solution.py:27
  355.5 428.4 %reduce-scatter.2.cloned.1.call-start = ((), (), s32[]{:S(2)}) async-start(), calls=%async_computation.4 | async-start | bytes 21626880 | tf_op jit(solution)/shard_map/reduce_scatter | solution.py:34
Sparse Core Ops, SparseCore 0:
  9.2 104.0 all-gather.7
  115.1 203.4 all-gather.9
  321.1 242.7 all-gather.5
  596.6 187.2 reduce-scatter.1
where the time goes:
time: 794 us; the launch traced here: 793 us
  waiting for transfers between devices  651 us (82%)
  local copies, waits for them, and re-layouts  64.4 us (8%)
  matrix products  34.3 us (4%)
  starting transfers between devices  21.5 us (3%)
  between operations  13.2 us (2%)
  other arithmetic  8.68 us (1%)
    all_gather x1, waiting for transfers between devices, local(): lax.all_gather(xin, 'mp', axis=0, tiled=True)  208 us
    reduce_scatter x1, waiting for transfers between devices, local(): lax.psum_scatter(jnp.dot(hidden, w_down, preferred_element_type=jnp.float...  187 us
    all_gather x1, waiting for transfers between devices, local(): down_columns = lax.all_gather(down_half, 'rep', axis=0, tiled=True)  158 us
    all_gather x1, waiting for transfers between devices, local(): up_rows = lax.all_gather(up_half, 'rep', axis=1, tiled=True)  96.8 us
    all_to_all x2, local copies, waits for them, and re-layouts, local(): lax.all_to_all(up_rows, 'mp', split_axis=1, concat_axis=0, tiled=True)  21.5 us
    all_to_all x2, local copies, waits for them, and re-layouts, local(): lax.all_to_all(down_columns, 'mp', split_axis=0, concat_axis=1, tiled=True)  18.6 us
    dot_general x1, matrix products, local(): jnp.dot(hidden, w_down, preferred_element_type=jnp.float32)  16.8 us
  transfers between devices with their start and end apart: 6, of which 4 were waited for; matrix products, arithmetic and copies ran while one was open for 8% of the time, Pallas kernels for 0%

commit v1 on v0

--- a/solution.py
+++ b/solution.py
@@ -27,7 +27,11 @@
     w_down = lax.all_to_all(down_columns, "mp", split_axis=0, concat_axis=1, tiled=True)
     hidden = jax.nn.gelu(
         jnp.dot(
-            lax.all_gather(xin, "mp", axis=0, tiled=True), w_up, preferred_element_type=jnp.float32
+            jnp.concatenate(
+                lax.all_to_all(jnp.stack([xin] * lax.axis_size("mp")), "mp", 0, 0), axis=0
+            ),
+            w_up,
+            preferred_element_type=jnp.float32,
         ),
         approximate=True,
     ).astype(jnp.bfloat16)

time: 794 us -> 1170 us (1.47)
  waiting for transfers between devices: 651 us -> 1020 us
    all_gather x1 -> x0, waiting for transfers between devices: 208 us -> none  [local(): lax.all_gather(xin, 'mp', axis=0, tiled=True)]
    all_gather x1, waiting for transfers between devices: 158 us -> 337 us  [local(): down_columns = lax.all_gather(down_half, 'rep', axis=0, tiled=True)]
    all_to_all x0 -> x1, waiting for transfers between devices: none -> 174 us  [local(): lax.all_to_all(jnp.stack([xin] * lax.axis_size('mp')), 'mp', 0, 0)]
    all_to_all x1, waiting for transfers between devices: 0.01 us -> 111 us  [local(): lax.all_to_all(up_rows, 'mp', split_axis=1, concat_axis=0, tiled=True)]
    all_to_all x1, waiting for transfers between devices: 0.01 us -> 100 us  [local(): lax.all_to_all(down_columns, 'mp', split_axis=0, concat_axis=1, tiled=True)]
  transfers between devices with their start and end apart: 6 -> 6, of which waited for: 4 -> 6; matrix products, arithmetic and copies ran while one was open for 8% -> 3% of each run, Pallas kernels for 0% -> 0%
where the time goes in v1:
time: 1170 us
  waiting for transfers between devices  1020 us (87%)
  local copies, waits for them, and re-layouts  71.3 us (6%)
  matrix products  34.2 us (3%)
  starting transfers between devices  30.1 us (3%)
  between operations  13.2 us (1%)
    all_gather x1, waiting for transfers between devices, local(): down_columns = lax.all_gather(down_half, 'rep', axis=0, tiled=True)  337 us
    reduce_scatter x1, waiting for transfers between devices, local(): lax.psum_scatter(jnp.dot(hidden, w_down, preferred_element_type=jnp.float...  191 us
    all_to_all x1, waiting for transfers between devices, local(): lax.all_to_all(jnp.stack([xin] * lax.axis_size('mp')), 'mp', 0, 0)  174 us
    all_to_all x1, waiting for transfers between devices, local(): lax.all_to_all(up_rows, 'mp', split_axis=1, concat_axis=0, tiled=True)  111 us
    all_gather x1, waiting for transfers between devices, local(): up_rows = lax.all_gather(up_half, 'rep', axis=1, tiled=True)  105 us
    all_to_all x1, waiting for transfers between devices, local(): lax.all_to_all(down_columns, 'mp', split_axis=0, concat_axis=1, tiled=True)  100 us
  transfers between devices with their start and end apart: 6, of which 6 were waited for; matrix products, arithmetic and copies ran while one was open for 3% of the time, Pallas kernels for 0%

profile of v1, /device:TPU:1, one launch (start us, length us, event | category | flops | bytes accessed | tf_op | source)
XLA Modules:
  0.0 1173.0 jit_solution(6402995862321753696)
XLA Ops:
  6.5 2.1 convert_bitcast_fusion.2
  8.7 104.6 %all-gather.5.cloned.1.call-done = bf16[8,1728,160]{1,2,0:T(8,128)(2,1)} async-done(((bf16[1,1728,160]{1,2,0:T(8,128)(2,1)}), bf16[8,1728,160]{1,2,0:T(8,128)(2,1)}) %all-gather.5.cloned.1.call-update) | async-done | bytes 4423696 | tf_op jit(solution)/shard_map/all_gather | solution.py:24
  113.3 6.9 copy.13
  120.2 8.6 reshape.53
  128.8 13.6 %all_to_all.32 = bf16[160,32,432]{2,1,0:T(8,128)(2,1)} reshape(bf16[160,13824]{1,0:T(8,128)(2,1)} %bitcast.78) | data formatting | bytes 8847360 | tf_op jit(solution)/shard_map/all_to_all | solution.py:25
  142.4 7.7 copy.14
  150.2 9.8 all-to-all-start.1
  160.6 1.8 fusion.24
  162.4 1.9 copy-done
  164.7 110.5 %all-to-all-done.1 = bf16[160,32,432]{2,0,1:T(8,128)(2,1)} async-done(((bf16[160,32,432]{2,0,1:T(8,128)(2,1)}), bf16[160,32,432]{2,0,1:T(8,128)(2,1)}, u32[]{:S(2)}, u32[]{:S(2)}) %all-to-all-start.1) | async-done | bytes 4423712 | tf_op jit(solution)/shard_map/all_to_all | solution.py:25
  275.2 7.4 stack.5
  282.6 9.5 all-to-all-start
  292.2 0.9 convert_bitcast_fusion.1
  293.0 337.5 %all-gather.7.cloned.1.call-done = bf16[8,1728,160]{1,2,0:T(8,128)(2,1)} async-done(((bf16[1,1728,160]{1,2,0:T(8,128)(2,1)}), bf16[8,1728,160]{1,2,0:T(8,128)(2,1)}) %all-gather.7.cloned.1.call-update) | async-done | bytes 4423696 | tf_op jit(solution)/shard_map/all_gather | solution.py:26
  630.5 6.9 copy.15
  637.4 10.6 all_to_all.36
  648.0 7.7 copy.16
  655.7 174.0 %all-to-all-done = bf16[32,64,5120]{2,1,0:T(8,128)(2,1)} async-done(((bf16[32,64,5120]{2,1,0:T(8,128)(2,1)}), bf16[32,64,5120]{2,1,0:T(8,128)(2,1)}, u32[]{:S(2)}, u32[]{:S(2)}) %all-to-all-start) | async-done | bytes 20971552 | tf_op jit(solution)/shard_map/all_to_all | solution.py:31
  829.7 10.4 all-to-all-start.2
  840.4 15.7 %fusion.50 = bf16[2048,432]{0,1:T(8,128)(2,1)S(1)} fusion(bf16[2048,5120]{1,0:T(8,128)(2,1)} %bitcast.8, bf16[5120,432]{1,0:T(8,128)(2,1)} %bitcast.13), kind=kOutput, calls=%fused_computation.9.clone.clone.1 | convolution fusion | flops 9067659264 | bytes 27164672 | tf_op jit(solution)/shard_map/dot_general | solution.py:29
  856.1 100.1 %all-to-all-done.2 = bf16[32,432,160]{1,2,0:T(8,128)(2,1)} async-done(((bf16[32,432,160]{1,2,0:T(8,128)(2,1)}), bf16[32,432,160]{1,2,0:T(8,128)(2,1)}, u32[]{:S(2)}, u32[]{:S(2)}) %all-to-all-start.2) | async-done | bytes 4423712 | tf_op jit(solution)/shard_map/all_to_all | solution.py:27
  956.2 16.8 %convolution_convert_fusion = bf16[2048,5120]{1,0:T(8,128)(2,1)} fusion(bf16[432,5120]{0,1:T(8,128)(2,1)} %bitcast.16, bf16[2048,432]{0,1:T(8,128)(2,1)S(1)} %fusion.50), kind=kOutput, calls=%fused_computation | convolution fusion | flops 9070182400 | bytes 27164672 | tf_op jit(solution)/shard_map/dot_general | solution.py:39
  973.0 190.9 %reduce-scatter.2.cloned.1.call-done = bf16[64,5120]{1,0:T(8,128)(2,1)} async-done(((bf16[2048,5120]{1,0:T(8,128)(2,1)}), bf16[64,5120]{1,0:T(8,128)(2,1)}) %reduce-scatter.2.cloned.1.call-update) | async-done | bytes 655376 | tf_op jit(solution)/shard_map/reduce_scatter | solution.py:38
  1163.9 2.6 fusion.27
  (20 shorter events, 1.3 us)
Async XLA Ops:
  6.5 106.8 %all-gather.5.cloned.1.call-start = ((), (), s32[]{:S(2)}) async-start(), calls=%async_computation.5 | async-start | bytes 5160960 | tf_op jit(solution)/shard_map/all_gather | solution.py:24
  150.2 9.9 copy-start.1
  150.2 10.4 copy-start.2
  150.2 10.4 copy-start.4
  150.2 125.0 %all-to-all-start.1 = ((bf16[160,32,432]{2,0,1:T(8,128)(2,1)}), bf16[160,32,432]{2,0,1:T(8,128)(2,1)}, u32[]{:S(2)}, u32[]{:S(2)}) async-start(bf16[160,32,432]{2,0,1:T(8,128)(2,1)} %copy.14), calls=%async_computation.1 | async-start | bytes 10485760 | tf_op jit(solution)/shard_map/all_to_all | solution.py:25
  162.4 1.9 copy-start
  282.6 9.6 copy-start.3
  282.6 547.1 %all-to-all-start = ((bf16[32,64,5120]{2,1,0:T(8,128)(2,1)}), bf16[32,64,5120]{2,1,0:T(8,128)(2,1)}, u32[]{:S(2)}, u32[]{:S(2)}) async-start(bf16[32,64,5120]{2,1,0:T(8,128)(2,1)} %stack.5), calls=%async_computation | async-start | bytes 41943040 | tf_op jit(solution)/shard_map/all_to_all | solution.py:31
  292.1 338.4 %all-gather.7.cloned.1.call-start = ((), (), s32[]{:S(2)}) async-start(), calls=%async_computation.6 | async-start | bytes 5160960 | tf_op jit(solution)/shard_map/all_gather | solution.py:26
  829.7 126.5 %all-to-all-start.2 = ((bf16[32,432,160]{1,2,0:T(8,128)(2,1)}), bf16[32,432,160]{1,2,0:T(8,128)(2,1)}, u32[]{:S(2)}, u32[]{:S(2)}) async-start(bf16[32,432,160]{1,2,0:T(8,128)(2,1)} %copy.16), calls=%async_computation.2 | async-start | bytes 10485760 | tf_op jit(solution)/shard_map/all_to_all | solution.py:27
  840.2 323.8 %reduce-scatter.2.cloned.1.call-start = ((), (), s32[]{:S(2)}) async-start(), calls=%async_computation.4 | async-start | bytes 21626880 | tf_op jit(solution)/shard_map/reduce_scatter | solution.py:38
Sparse Core Ops, SparseCore 0:
  9.1 104.0 all-gather.4
  294.7 335.7 all-gather.6
  973.1 190.7 reduce-scatter.1
